TPU v7x, 128 devices: a whole 4x4x4 slice. The times are simulated.
128 devices in a mesh: gx: 16 (over x, y_hi, core), gy: 8 (over y_lo, z).
Axes of the slice: x: 4, y: 4 (y_hi: 2, y_lo: 2; y = y_hi * 2 + y_lo), z: 4, core: 2. Of those that a mesh axis runs over, the one named last changes fastest.
Arguments:
- right_side: float32 [512, 256, 512], P('gx', 'gy'), may hold values from -24 to 24
- alpha_coef: float32 [512, 256, 512], P('gx', 'gy'), may hold values from 0.05 to 0.5
- face_coef: float32 [3, 512, 256, 512], P(None, 'gx', 'gy'), may hold values from 0.25 to 4
- owner_map: int32 [8, 256], P('gy'), may hold values from 0 to 15, as said below
Outputs:
- solution: float32 [512, 256, 512], P('gx', 'gy')
- coarse_residual: float32 [256, 128, 256], P('gx', 'gy')
- coarse_coef: float32 [4, 256, 128, 256], P(None, 'gx', 'gy')
Inputs may be any that keep to these rules, and one draw needn't show every extreme that they name: `owner_map`: each row's tiles are cut by recursive bisection into boxes of 4 x 4 tiles, one box to each owner; every device that sends to an owner sends it exactly 4 tiles.
All inputs are finite; a program needn't handle non-finite values.
Results may differ from a plain program's by a relative error of at most 0.00002.
Values sent between devices are 32-bit elements; how exact they have to be, the bound alone decides.
A program may use at most 192 MiB of HBM per device.

v0:
```python
import jax
import jax.numpy as jnp
from jax import lax
from jax.sharding import PartitionSpec as P

SIDE = 4
ITERS = 4


cheb_high = 2.0
cheb_low = 0.25


def padded_2(cells, sides, width):
    for axis, dim in sides:
        count = lax.axis_size(axis)
        ends = count - 1
        head = lax.slice_in_dim(cells, 0, width, axis=dim)
        tail = lax.slice_in_dim(cells, cells.shape[dim] - width, cells.shape[dim], axis=dim)
        cells = jnp.concatenate(
            [
                lax.ppermute(tail, axis, [(i, (i + 1) % count) for i in range(ends)]),
                cells,
                lax.ppermute(head, axis, [((i + 1) % count, i) for i in range(ends)]),
            ],
            axis=dim,
        )
    return cells


def passed_along(block, axis, distance):
    devices = range(lax.axis_size(axis))
    route = [(i - distance, i) for i in devices if i - distance in devices]
    return lax.ppermute(block, axis, route)


def shift_lower(field):
    return jnp.concatenate([jnp.zeros_like(field[..., :1]), field[..., :-1]], axis=-1)


def shift_upper(field):
    return jnp.concatenate([field[..., 1:], jnp.zeros_like(field[..., :1])], axis=-1)


def apply_operator(padded, alpha_inner, faces_padded):
    center = padded[1:-1, 1:-1]
    face_x = faces_padded[0, 1:-1, 1:-1]
    face_xu = faces_padded[0, 2:, 1:-1]
    face_y = faces_padded[1, 1:-1, 1:-1]
    face_yu = faces_padded[1, 1:-1, 2:]
    face_z = faces_padded[2, 1:-1, 1:-1]
    face_zu = shift_upper(face_z)
    result = alpha_inner * center
    result = result + face_x * (center - padded[:-2, 1:-1]) + face_xu * (center - padded[2:, 1:-1])
    result = result + face_y * (center - padded[1:-1, :-2]) + face_yu * (center - padded[1:-1, 2:])
    result = (
        result + face_z * (center - shift_lower(center)) + face_zu * (center - shift_upper(center))
    )
    return result


def diagonal_of(alpha_inner, faces_padded):
    face_x = faces_padded[0, 1:-1, 1:-1]
    face_xu = faces_padded[0, 2:, 1:-1]
    face_y = faces_padded[1, 1:-1, 1:-1]
    face_yu = faces_padded[1, 1:-1, 2:]
    face_z = faces_padded[2, 1:-1, 1:-1]
    return alpha_inner + face_x + face_xu + face_y + face_yu + face_z + shift_upper(face_z)


def chebyshev_constants():
    theta_mid = (cheb_high + cheb_low) / 2.0
    delta_half = (cheb_high - cheb_low) / 2.0
    return (theta_mid, delta_half, theta_mid / delta_half)


def field_with_rim(field):
    return padded_2(field, (("gx", 0), ("gy", 1)), 1)


def faces_with_next(face_coef):
    next_x = passed_along(face_coef[0, :1], "gx", -1)
    next_y = passed_along(face_coef[1, :, :1], "gy", -1)
    padded_x = jnp.pad(jnp.concatenate([face_coef[0], next_x], axis=0), ((1, 0), (1, 1), (0, 0)))
    padded_y = jnp.pad(jnp.concatenate([face_coef[1], next_y], axis=1), ((1, 1), (1, 0), (0, 0)))
    padded_z = jnp.pad(face_coef[2], ((1, 1), (1, 1), (0, 0)))
    return jnp.stack([padded_x, padded_y, padded_z], axis=0)


def smooth_each(right_side, alpha_coef, face_coef):
    theta_mid, delta_half, sigma_ratio = chebyshev_constants()
    faces_padded = faces_with_next(face_coef)
    inverse = 1.0 / diagonal_of(alpha_coef, faces_padded)
    solution = inverse * right_side / theta_mid
    update = solution
    rho_prev = 1.0 / sigma_ratio
    for _ in range(ITERS - 1):
        residual = right_side - apply_operator(field_with_rim(solution), alpha_coef, faces_padded)
        rho_next = 1.0 / (2.0 * sigma_ratio - rho_prev)
        update = rho_next * rho_prev * update + 2.0 * rho_next / delta_half * inverse * residual
        solution = solution + update
        rho_prev = rho_next
    residual = right_side - apply_operator(field_with_rim(solution), alpha_coef, faces_padded)
    return (solution, residual)


def pair_sum_z(field):
    return field[..., 0::2] + field[..., 1::2]


def split_major(field):
    return field.reshape(field.shape[0] // 2, 2, field.shape[1] // 2, 2, field.shape[2])


def average_cells(field):
    return jnp.sum(split_major(pair_sum_z(field)), axis=(1, 3)) * 0.125


def average_faces(faces):
    along_x = jnp.sum(split_major(pair_sum_z(faces[0]))[:, 0], axis=2) * 0.25
    along_y = jnp.sum(split_major(pair_sum_z(faces[1]))[:, :, :, 0], axis=1) * 0.25
    along_z = jnp.sum(split_major(faces[2][..., 0::2]), axis=(1, 3)) * 0.25
    return [along_x, along_y, along_z]


def coarse_tiles(coarse, tiles_dev):
    half_cells = coarse.shape[0]
    shaped = coarse.reshape(coarse.shape[0], coarse.shape[1], tiles_dev, half_cells)
    return shaped.transpose(2, 1, 0, 3).reshape(tiles_dev, half_cells, half_cells * half_cells)


def send_slots(owner_row, device_x, devices_x, tiles_dev):
    mine = lax.dynamic_slice_in_dim(owner_row, device_x * tiles_dev, tiles_dev)
    tile_index = jnp.arange(tiles_dev, dtype=jnp.int32)
    earlier = tile_index[None, :] < tile_index[:, None]
    same_owner = mine[None, :] == mine[:, None]
    order_rank = jnp.sum((earlier & same_owner).astype(jnp.int32), axis=1)
    slot_index = jnp.arange(devices_x * SIDE, dtype=jnp.int32)
    target = slot_index // SIDE
    within = slot_index % SIDE
    matches = (mine[None, :] == target[:, None]) & (order_rank[None, :] == within[:, None])
    picked = jnp.sum(jnp.where(matches, tile_index[None, :], 0), axis=1)
    used = jnp.any(matches, axis=1)
    return (picked, used)


def receive_slots(owner_row, device_x, tiles_dev):
    owned = owner_row == device_x
    tile_ids = jnp.arange(owner_row.shape[0], dtype=jnp.int32)
    position = jnp.cumsum(owned.astype(jnp.int32)) - 1
    wanted = jnp.arange(tiles_dev, dtype=jnp.int32)
    selected = owned[None, :] & (position[None, :] == wanted[:, None])
    chosen_id = jnp.sum(jnp.where(selected, tile_ids[None, :], 0), axis=1)
    source = chosen_id // tiles_dev
    before = jnp.sum(
        (owned[None, :] & (tile_ids[None, :] < (source * tiles_dev)[:, None])).astype(jnp.int32),
        axis=1,
    )
    return source * SIDE + wanted - before


def pack_tiles(tiles, picked, used):
    gathered = jnp.take(tiles, picked, axis=1)
    return jnp.where(used[None, :, None, None], gathered, 0.0)


def local(right_side, alpha_coef, face_coef, owner_map):
    cells = right_side.shape[0]
    tiles_dev = right_side.shape[2] // cells
    devices_x = lax.axis_size("gx")
    device_x = lax.axis_index("gx")
    owner_row = owner_map[0]
    picked, used = send_slots(owner_row, device_x, devices_x, tiles_dev)
    arrival = receive_slots(owner_row, device_x, tiles_dev)
    fields = [average_cells(alpha_coef)] + average_faces(face_coef)
    coef_tiles = jnp.stack([coarse_tiles(field, tiles_dev) for field in fields], axis=0)
    coef_send = pack_tiles(coef_tiles, picked, used)
    solution, residual = smooth_each(right_side, alpha_coef, face_coef)
    residual_tiles = coarse_tiles(average_cells(residual), tiles_dev)[None]
    residual_send = pack_tiles(residual_tiles, picked, used)
    residual_back, coef_back = (
        lax.all_to_all(residual_send, "gx", split_axis=1, concat_axis=1, tiled=True),
        lax.all_to_all(coef_send, "gx", split_axis=1, concat_axis=1, tiled=True),
    )
    coarse_residual = jnp.take(residual_back[0], arrival, axis=0)
    coarse_coef = jnp.take(coef_back, arrival, axis=1)
    return (solution, coarse_residual, coarse_coef)


def solution(mesh):
    return jax.shard_map(
        local,
        mesh=mesh,
        in_specs=(
            P("gx", "gy", None),
            P("gx", "gy", None),
            P(None, "gx", "gy", None),
            P("gy", None),
        ),
        out_specs=(P("gx", "gy", None), P("gx", "gy", None), P(None, "gx", "gy", None)),
        check_vma=False,
    )
```

profile of v0, /device:TPU:29, one launch (start us, length us, event | category | flops | bytes accessed | tf_op | source)
XLA Modules:
  0.0 653.5 jit_solution(1038996379201672666)
XLA Ops:
  1.7 2.6 collective-permute-start
  5.4 5.8 collective-permute-start.1
  11.3 36.5 %slice.292 = f32[32,32,256]{2,1,0:T(8,128)} slice(f32[32,32,512]{2,1,0:T(8,128)} %param.5), slice={[0:32:1], [0:32:1], [1:512:2]} | slice | bytes 2097152 | tf_op jit(solution)/shard_map/slice | solution.py:108
  47.7 35.6 %slice.291 = f32[32,32,256]{2,1,0:T(8,128)} slice(f32[32,32,512]{2,1,0:T(8,128)S(1)} %copy-done.6), slice={[0:32:1], [0:32:1], [0:512:2]} | slice | bytes 2097152 | tf_op jit(solution)/shard_map/slice | solution.py:108
  83.4 6.0 fusion.87
  90.6 35.3 %slice.294 = f32[32,32,256]{2,0,1:T(8,128)S(1)} slice(f32[32,32,512]{2,0,1:T(8,128)S(1)} %bitcast.155), slice={[0:32:1], [0:32:1], [1:512:2]} | slice | bytes 2097152 | tf_op jit(solution)/shard_map/slice | solution.py:108
  125.9 36.0 %slice.293 = f32[32,32,256]{2,0,1:T(8,128)} slice(f32[32,32,512]{2,0,1:T(8,128)S(1)} %bitcast.156), slice={[0:32:1], [0:32:1], [0:512:2]} | slice | bytes 2097152 | tf_op jit(solution)/shard_map/slice | solution.py:108
  165.6 2.0 reduce_sum.95
  169.6 2.0 reshape.220
  173.0 4.0 copy_bitcast_fusion
  179.5 2.2 copy-done.17
  184.4 7.7 %broadcast_multiply_fusion = (f32[32,32,512]{2,0,1:T(8,128)S(1)}, f32[32,32,512]{2,0,1:T(8,128)}) fusion(f32[32,32,512]{2,1,0:T(8,128)S(1)} %copy-done.14, f32[32,32,511]{2,0,1:T(8,128)S(1)} %slice.313, f32[1,34,34,512]{3,1,2,0:T(8,128)S(1)} %pad_bitcast_fusion, f32[1,34,34,512]{3,1,2,0:T(8,128)S(1)} %fusion.2, f32[1,34,34,512]{3,1,2,0:T(8,128)S(1)} %fusion.3, ...), kind=kLoop, calls=%fused_computation.132 | loop fusion | flops 4718592 | bytes 20967424 | tf_op jit(solution)/shard_map/div | solution.py:94
  192.2 6.3 collective-permute-start.2
  198.5 1.9 collective-permute-start.3
  200.4 6.0 collective-permute-done.3
  206.5 2.1 collective-permute-start.4
  208.6 5.5 collective-permute-start.5
  214.0 2.7 fusion.95
  216.8 15.2 %fusion.76 = (f32[32,32,512]{2,0,1:T(8,128)}, f32[32,32,512]{2,0,1:T(8,128)}) fusion(f32[32,32,512]{2,0,1:T(8,128)} %get-tuple-element.28, f32[32,32,512]{2,0,1:T(8,128)} %copy-done.12, f32[32,32,511]{2,0,1:T(8,128)} %get-tuple-element.55, f32[32,32,511]{2,0,1:T(8,128)} %get-tuple-element.54, f32[34,1,512]{2,0,1:T(8,128)S(1)} %collective-permute-done.5, ...), kind=kLoop, calls=%fused_computation.133 | loop fusion | flops 21495808 | bytes 29618176 | tf_op jit(solution)/shard_map/add | solution.py:101
  233.3 2.4 collective-permute-start.6
  235.8 1.9 collective-permute-start.7
  237.7 36.5 %slice.299 = f32[32,32,256]{2,0,1:T(8,128)} slice(f32[32,32,512]{2,0,1:T(8,128)} %copy-done.20), slice={[0:32:1], [0:32:1], [0:512:2]} | slice | bytes 2097152 | tf_op jit(solution)/shard_map/slice | solution.py:122
  274.2 2.9 reshape.222
  277.1 2.0 reduce_sum.98
  280.2 1.9 collective-permute-start.8
  282.1 6.0 collective-permute-start.9
  288.1 5.1 fusion.93
  293.2 15.0 %fusion.83 = (f32[32,32,512]{2,0,1:T(8,128)}, f32[32,32,512]{2,0,1:T(8,128)}) fusion(f32[32,32,512]{2,0,1:T(8,128)} %get-tuple-element.25, f32[32,32,511]{2,0,1:T(8,128)} %get-tuple-element.51, f32[32,32,511]{2,0,1:T(8,128)} %get-tuple-element.50, f32[34,1,512]{2,0,1:T(8,128)S(1)} %collective-permute-done.9, f32[1,32,512]{2,0,1:T(1,128)S(1)} %collective-permute-done.7, ...), kind=kLoop, calls=%fused_computation.199 | loop fusion | flops 20971520 | bytes 29618176 | tf_op jit(solution)/shard_map/add | solution.py:101
  309.7 6.6 %collective-permute-start.10 = (f32[1,32,512]{2,0,1:T(1,128)S(1)}, f32[1,32,512]{2,0,1:T(1,128)S(1)}, u32[]{:S(2)}, u32[]{:S(2)}) collective-permute-start(f32[1,32,512]{2,0,1:T(1,128)S(1)} %get-tuple-element.46), channel_id=1, source_target_pairs={{0,8},{8,16},{16,24},{24,32},{32,40},{40,48},{48,56},{56,64},{64,7... | collective-permute-start | bytes 196616 | tf_op jit(solution)/shard_map/ppermute | solution.py:22
  316.3 1.9 collective-permute-start.11
  318.3 6.0 collective-permute-done.11
  325.2 1.9 collective-permute-start.12
  327.1 5.5 collective-permute-start.13
  332.6 2.8 fusion.90
  335.4 13.9 %fusion.29 = f32[32,32,512]{2,0,1:T(8,128)S(1)} fusion(f32[32,32,512]{2,0,1:T(8,128)} %get-tuple-element.23, f32[34,1,512]{2,0,1:T(8,128)S(1)} %collective-permute-done.13, f32[1,32,512]{2,0,1:T(1,128)S(1)} %collective-permute-done.11, f32[1,32,512]{2,0,1:T(1,128)S(1)} %collective-permute-done.10, f32[34,1,512]{2,0,1:T(8,128)S(1)} %collective-permute-done.12, ...), kind=kLoop, calls=%fused_computation.50 | loop fusion | flops 20971520 | bytes 27521024 | tf_op jit(solution)/shard_map/add | solution.py:101
  349.5 2.4 collective-permute-start.14
  351.9 1.9 collective-permute-start.15
  353.9 6.0 collective-permute-done.15
  359.9 1.9 collective-permute-start.16
  361.9 5.7 collective-permute-start.17
  367.6 2.8 fusion.88
  370.5 12.2 %fusion.11 = f32[32,32,512]{2,0,1:T(8,128)} fusion(f32[32,32,512]{2,0,1:T(8,128)S(1)} %fusion.29, f32[34,1,512]{2,0,1:T(8,128)S(1)} %collective-permute-done.17, f32[1,32,512]{2,0,1:T(1,128)S(1)} %collective-permute-done.15, f32[1,32,512]{2,0,1:T(1,128)S(1)} %collective-permute-done.14, f32[34,1,512]{2,0,1:T(8,128)S(1)} %collective-permute-done.16, ...), kind=kLoop, calls=%fused_computation.24 | loop fusion | flops 14680064 | bytes 25423872 | tf_op jit(solution)/shard_map/sub | solution.py:103
  382.7 36.0 %slice.290 = f32[32,32,256]{2,0,1:T(8,128)S(1)} slice(f32[32,32,512]{2,0,1:T(8,128)} %fusion.11), slice={[0:32:1], [0:32:1], [1:512:2]} | slice | bytes 2097152 | tf_op jit(solution)/shard_map/slice | solution.py:108
  418.8 35.8 %slice.289 = f32[32,32,256]{2,0,1:T(8,128)} slice(f32[32,32,512]{2,0,1:T(8,128)S(1)} %copy-done.21), slice={[0:32:1], [0:32:1], [0:512:2]} | slice | bytes 2097152 | tf_op jit(solution)/shard_map/slice | solution.py:108
  458.2 2.6 copy.117
  460.8 2.4 reshape.224
  465.0 7.0 %all-to-all-start = ((f32[1,64,16,256]{3,2,0,1:T(8,128)}), f32[1,64,16,256]{3,2,0,1:T(8,128)}, u32[]{:S(2)}, u32[]{:S(2)}) async-start(f32[1,64,16,256]{3,2,0,1:T(8,128)} %fusion.75), calls=%async_computation | async-start | bytes 2097152 | tf_op jit(solution)/shard_map/all_to_all | solution.py:182
  472.7 35.1 %slice.297 = f32[32,32,256]{2,0,1:T(8,128)S(1)} slice(f32[32,32,512]{2,0,1:T(8,128)S(1)} %copy-done.19), slice={[0:32:1], [0:32:1], [1:512:2]} | slice | bytes 2097152 | tf_op jit(solution)/shard_map/slice | solution.py:108
  507.8 35.6 %slice.296 = f32[32,32,256]{2,0,1:T(8,128)} slice(f32[32,32,512]{2,0,1:T(8,128)S(1)} %copy-done.19), slice={[0:32:1], [0:32:1], [0:512:2]} | slice | bytes 2097152 | tf_op jit(solution)/shard_map/slice | solution.py:108
  545.2 2.6 copy.121
  547.8 3.1 stack_reshape.12
  551.7 2.6 copy.123
  554.3 3.3 stack_reshape.13
  560.0 2.6 copy.125
  562.5 2.4 stack_reshape.14
  565.6 2.6 copy.127
  568.2 2.5 stack_reshape.15
  570.8 2.8 gather_fusion.2
  573.6 4.7 select_bitcast_fusion
  578.3 7.4 %all-to-all-start.1 = ((f32[4,64,16,256]{3,2,0,1:T(8,128)}), f32[4,64,16,256]{3,2,0,1:T(8,128)}, u32[]{:S(2)}, u32[]{:S(2)}) async-start(f32[4,64,16,256]{3,2,0,1:T(8,128)} %select_bitcast_fusion), calls=%async_computation.1 | async-start | bytes 8388608 | tf_op jit(solution)/shard_map/all_to_all | solution.py:183
  586.7 2.5 copy.129
  591.8 52.5 %all-to-all-done.1 = f32[4,64,16,256]{3,2,0,1:T(8,128)} async-done(((f32[4,64,16,256]{3,2,0,1:T(8,128)}), f32[4,64,16,256]{3,2,0,1:T(8,128)}, u32[]{:S(2)}, u32[]{:S(2)}) %all-to-all-start.1) | async-done | bytes 4194336 | tf_op jit(solution)/shard_map/all_to_all | solution.py:183
  644.3 4.8 copy.128
  649.1 2.8 gather_fusion.3
  (145 shorter events, 37.0 us)
Async XLA Ops:
  0.6 47.1 %copy-start.6 = (f32[32,32,512]{2,1,0:T(8,128)S(1)}, f32[32,32,512]{2,1,0:T(8,128)}, u32[]{:S(2)}) copy-start(f32[32,32,512]{2,1,0:T(8,128)} %param.5) | copy-start | bytes 6291460
  1.7 177.8 %collective-permute-start = (f32[1,32,512]{2,0,1:T(1,128)S(1)}, f32[1,32,512]{2,0,1:T(1,128)S(1)}, u32[]{:S(2)}, u32[]{:S(2)}) collective-permute-start(f32[1,32,512]{2,0,1:T(1,128)S(1)} %bitcast.163), channel_id=1, source_target_pairs={{8,0},{16,8},{24,16},{32,24},{40,32},{48,40},{56,48},{64,56},{72,6... | collective-permute-start | bytes 196616 | tf_op jit(solution)/shard_map/ppermute | solution.py:34
  5.4 176.8 %collective-permute-start.1 = (f32[32,1,512]{2,0,1:T(8,128)S(1)}, f32[32,1,512]{2,0,1:T(8,128)S(1)}, u32[]{:S(2)}, u32[]{:S(2)}) collective-permute-start(f32[32,1,512]{2,0,1:T(8,128)S(1)} %bitcast.164), channel_id=1, source_target_pairs={{1,0},{2,1},{3,2},{4,3},{5,4},{6,5},{7,6},{9,8},{10,9},{11,10},{12... | collective-permute-start | bytes 196616 | tf_op jit(solution)/shard_map/ppermute | solution.py:34
  90.6 71.4 %copy-start.16 = (f32[1,32,32,512]{3,1,2,0:T(8,128)}, f32[1,32,32,512]{3,1,2,0:T(8,128)S(1)}, u32[]{:S(2)}) copy-start(f32[1,32,32,512]{3,1,2,0:T(8,128)S(1)} %copy.158) | copy-start | bytes 6291460
  90.6 71.4 %copy-start.29 = (s32[1,256]{1,0:T(1,128)S(1)}, s32[1,256]{1,0:T(1,128)}, u32[]{:S(2)}) copy-start(s32[1,256]{1,0:T(1,128)} %param.7) | copy-start | bytes 3076
  163.9 4.5 copy-start.23
  169.6 3.5 copy-start.22
  177.1 1.4 copy-start.20
  177.1 5.1 copy-start.18
  178.4 38.3 %copy-start.2 = (f32[1,34,34,512]{3,1,2,0:T(8,128)}, f32[1,34,34,512]{3,1,2,0:T(8,128)S(1)}, u32[]{:S(2)}) copy-start(f32[1,34,34,512]{3,1,2,0:T(8,128)S(1)} %pad_bitcast_fusion) | copy-start | bytes 7102468
  178.8 2.9 copy-start.17
  179.4 37.4 %copy-start.9 = (f32[32,32,511]{2,0,1:T(8,128)}, f32[32,32,511]{2,0,1:T(8,128)S(1)}, u32[]{:S(2)}) copy-start(f32[32,32,511]{2,0,1:T(8,128)S(1)} %slice.313) | copy-start | bytes 6279172
  182.2 1.6 copy-start.7
  182.2 2.2 copy-start.14
  184.4 32.4 %copy-start = (f32[1,34,34,512]{3,1,2,0:T(8,128)}, f32[1,34,34,512]{3,1,2,0:T(8,128)S(1)}, u32[]{:S(2)}) copy-start(f32[1,34,34,512]{3,1,2,0:T(8,128)S(1)} %fusion.2) | copy-start | bytes 7102468
  192.1 24.7 %copy-start.12 = (f32[32,32,512]{2,0,1:T(8,128)}, f32[32,32,512]{2,0,1:T(8,128)S(1)}, u32[]{:S(2)}) copy-start(f32[32,32,512]{2,0,1:T(8,128)S(1)} %get-tuple-element.27) | copy-start | bytes 6291460
  192.2 8.2 %collective-permute-start.2 = (f32[1,32,512]{2,0,1:T(1,128)S(1)}, f32[1,32,512]{2,0,1:T(1,128)S(1)}, u32[]{:S(2)}, u32[]{:S(2)}) collective-permute-start(f32[1,32,512]{2,0,1:T(1,128)S(1)} %get-tuple-element.52), channel_id=1, source_target_pairs={{0,8},{8,16},{16,24},{24,32},{32,40},{40,48},{48,56},{56,64},{64,7... | collective-permute-start | bytes 196616 | tf_op jit(solution)/shard_map/ppermute | solution.py:22
  198.5 8.0 %collective-permute-start.3 = (f32[1,32,512]{2,0,1:T(1,128)S(1)}, f32[1,32,512]{2,0,1:T(1,128)S(1)}, u32[]{:S(2)}, u32[]{:S(2)}) collective-permute-start(f32[1,32,512]{2,0,1:T(1,128)S(1)} %get-tuple-element.53), channel_id=1, source_target_pairs={{8,0},{16,8},{24,16},{32,24},{40,32},{48,40},{56,48},{64,56},{72,6... | collective-permute-start | bytes 196616 | tf_op jit(solution)/shard_map/ppermute | solution.py:24
  206.5 10.3 %collective-permute-start.4 = (f32[34,1,512]{2,0,1:T(8,128)S(1)}, f32[34,1,512]{2,0,1:T(8,128)S(1)}, u32[]{:S(2)}, u32[]{:S(2)}) collective-permute-start(f32[34,1,512]{2,0,1:T(8,128)S(1)} %get-tuple-element.38), channel_id=1, source_target_pairs={{0,1},{1,2},{2,3},{3,4},{4,5},{5,6},{6,7},{8,9},{9,10},{10,11},{11... | collective-permute-start | bytes 208904 | tf_op jit(solution)/shard_map/ppermute | solution.py:22
  208.6 8.2 %collective-permute-start.5 = (f32[34,1,512]{2,0,1:T(8,128)S(1)}, f32[34,1,512]{2,0,1:T(8,128)S(1)}, u32[]{:S(2)}, u32[]{:S(2)}) collective-permute-start(f32[34,1,512]{2,0,1:T(8,128)S(1)} %get-tuple-element.39), channel_id=1, source_target_pairs={{1,0},{2,1},{3,2},{4,3},{5,4},{6,5},{7,6},{9,8},{10,9},{11,10},{12... | collective-permute-start | bytes 208904 | tf_op jit(solution)/shard_map/ppermute | solution.py:24
  233.3 45.7 %collective-permute-start.6 = (f32[1,32,512]{2,0,1:T(1,128)S(1)}, f32[1,32,512]{2,0,1:T(1,128)S(1)}, u32[]{:S(2)}, u32[]{:S(2)}) collective-permute-start(f32[1,32,512]{2,0,1:T(1,128)S(1)} %get-tuple-element.48), channel_id=1, source_target_pairs={{0,8},{8,16},{16,24},{24,32},{32,40},{40,48},{48,56},{56,64},{64,7... | collective-permute-start | bytes 196616 | tf_op jit(solution)/shard_map/ppermute | solution.py:22
  235.8 43.3 %collective-permute-start.7 = (f32[1,32,512]{2,0,1:T(1,128)S(1)}, f32[1,32,512]{2,0,1:T(1,128)S(1)}, u32[]{:S(2)}, u32[]{:S(2)}) collective-permute-start(f32[1,32,512]{2,0,1:T(1,128)S(1)} %get-tuple-element.49), channel_id=1, source_target_pairs={{8,0},{16,8},{24,16},{32,24},{40,32},{48,40},{56,48},{64,56},{72,6... | collective-permute-start | bytes 196616 | tf_op jit(solution)/shard_map/ppermute | solution.py:24
  279.1 14.1 %copy-start.10 = (f32[32,32,511]{2,0,1:T(8,128)S(1)}, f32[32,32,511]{2,0,1:T(8,128)}, u32[]{:S(2)}) copy-start(f32[32,32,511]{2,0,1:T(8,128)} %copy-done.9) | copy-start | bytes 6279172
  280.2 13.0 %collective-permute-start.8 = (f32[34,1,512]{2,0,1:T(8,128)S(1)}, f32[34,1,512]{2,0,1:T(8,128)S(1)}, u32[]{:S(2)}, u32[]{:S(2)}) collective-permute-start(f32[34,1,512]{2,0,1:T(8,128)S(1)} %get-tuple-element.36), channel_id=1, source_target_pairs={{0,1},{1,2},{2,3},{3,4},{4,5},{5,6},{6,7},{8,9},{9,10},{10,11},{11... | collective-permute-start | bytes 208904 | tf_op jit(solution)/shard_map/ppermute | solution.py:22
  282.1 11.1 %copy-start.3 = (f32[1,34,34,512]{3,1,2,0:T(8,128)S(1)}, f32[1,34,34,512]{3,1,2,0:T(8,128)}, u32[]{:S(2)}) copy-start(f32[1,34,34,512]{3,1,2,0:T(8,128)} %copy-done.2) | copy-start | bytes 7102468
  282.1 11.1 %copy-start.8 = (f32[32,32,512]{2,1,0:T(8,128)S(1)}, f32[32,32,512]{2,1,0:T(8,128)}, u32[]{:S(2)}) copy-start(f32[32,32,512]{2,1,0:T(8,128)} %param.5) | copy-start | bytes 6291460
  282.1 11.1 %collective-permute-start.9 = (f32[34,1,512]{2,0,1:T(8,128)S(1)}, f32[34,1,512]{2,0,1:T(8,128)S(1)}, u32[]{:S(2)}, u32[]{:S(2)}) collective-permute-start(f32[34,1,512]{2,0,1:T(8,128)S(1)} %get-tuple-element.37), channel_id=1, source_target_pairs={{1,0},{2,1},{3,2},{4,3},{5,4},{6,5},{7,6},{9,8},{10,9},{11,10},{12... | collective-permute-start | bytes 208904 | tf_op jit(solution)/shard_map/ppermute | solution.py:24
  288.1 5.1 copy-start.1
  308.2 24.4 %copy-start.13 = (f32[32,32,512]{2,0,1:T(8,128)S(1)}, f32[32,32,512]{2,0,1:T(8,128)}, u32[]{:S(2)}) copy-start(f32[32,32,512]{2,0,1:T(8,128)} %get-tuple-element.23) | copy-start | bytes 6291460
  309.7 8.6 %collective-permute-start.10 = (f32[1,32,512]{2,0,1:T(1,128)S(1)}, f32[1,32,512]{2,0,1:T(1,128)S(1)}, u32[]{:S(2)}, u32[]{:S(2)}) collective-permute-start(f32[1,32,512]{2,0,1:T(1,128)S(1)} %get-tuple-element.46), channel_id=1, source_target_pairs={{0,8},{8,16},{16,24},{24,32},{32,40},{40,48},{48,56},{56,64},{64,7... | collective-permute-start | bytes 196616 | tf_op jit(solution)/shard_map/ppermute | solution.py:22
  316.3 8.0 %collective-permute-start.11 = (f32[1,32,512]{2,0,1:T(1,128)S(1)}, f32[1,32,512]{2,0,1:T(1,128)S(1)}, u32[]{:S(2)}, u32[]{:S(2)}) collective-permute-start(f32[1,32,512]{2,0,1:T(1,128)S(1)} %get-tuple-element.47), channel_id=1, source_target_pairs={{8,0},{16,8},{24,16},{32,24},{40,32},{48,40},{56,48},{64,56},{72,6... | collective-permute-start | bytes 196616 | tf_op jit(solution)/shard_map/ppermute | solution.py:24
  325.2 10.2 %collective-permute-start.12 = (f32[34,1,512]{2,0,1:T(8,128)S(1)}, f32[34,1,512]{2,0,1:T(8,128)S(1)}, u32[]{:S(2)}, u32[]{:S(2)}) collective-permute-start(f32[34,1,512]{2,0,1:T(8,128)S(1)} %get-tuple-element.34), channel_id=1, source_target_pairs={{0,1},{1,2},{2,3},{3,4},{4,5},{5,6},{6,7},{8,9},{9,10},{10,11},{11... | collective-permute-start | bytes 208904 | tf_op jit(solution)/shard_map/ppermute | solution.py:22
  327.1 8.3 %collective-permute-start.13 = (f32[34,1,512]{2,0,1:T(8,128)S(1)}, f32[34,1,512]{2,0,1:T(8,128)S(1)}, u32[]{:S(2)}, u32[]{:S(2)}) collective-permute-start(f32[34,1,512]{2,0,1:T(8,128)S(1)} %get-tuple-element.35), channel_id=1, source_target_pairs={{1,0},{2,1},{3,2},{4,3},{5,4},{6,5},{7,6},{9,8},{10,9},{11,10},{12... | collective-permute-start | bytes 208904 | tf_op jit(solution)/shard_map/ppermute | solution.py:24
  349.4 21.1 %copy-start.4 = (f32[32,32,512]{2,0,1:T(8,128)}, f32[32,32,512]{2,0,1:T(8,128)S(1)}, u32[]{:S(2)}) copy-start(f32[32,32,512]{2,0,1:T(8,128)S(1)} %fusion.29) | copy-start | bytes 6291460
  349.5 4.4 collective-permute-start.14
  351.9 8.0 %collective-permute-start.15 = (f32[1,32,512]{2,0,1:T(1,128)S(1)}, f32[1,32,512]{2,0,1:T(1,128)S(1)}, u32[]{:S(2)}, u32[]{:S(2)}) collective-permute-start(f32[1,32,512]{2,0,1:T(1,128)S(1)} %get-tuple-element.43), channel_id=1, source_target_pairs={{8,0},{16,8},{24,16},{32,24},{40,32},{48,40},{56,48},{64,56},{72,6... | collective-permute-start | bytes 196616 | tf_op jit(solution)/shard_map/ppermute | solution.py:24
  359.9 10.5 %collective-permute-start.16 = (f32[34,1,512]{2,0,1:T(8,128)S(1)}, f32[34,1,512]{2,0,1:T(8,128)S(1)}, u32[]{:S(2)}, u32[]{:S(2)}) collective-permute-start(f32[34,1,512]{2,0,1:T(8,128)S(1)} %get-tuple-element.32), channel_id=1, source_target_pairs={{0,1},{1,2},{2,3},{3,4},{4,5},{5,6},{6,7},{8,9},{9,10},{10,11},{11... | collective-permute-start | bytes 208904 | tf_op jit(solution)/shard_map/ppermute | solution.py:22
  361.9 8.6 %copy-start.11 = (f32[32,32,511]{2,0,1:T(8,128)S(1)}, f32[32,32,511]{2,0,1:T(8,128)}, u32[]{:S(2)}) copy-start(f32[32,32,511]{2,0,1:T(8,128)} %copy-done.9) | copy-start | bytes 6279172
  361.9 8.6 %copy-start.15 = (f32[32,32,512]{2,1,0:T(8,128)S(1)}, f32[32,32,512]{2,1,0:T(8,128)}, u32[]{:S(2)}) copy-start(f32[32,32,512]{2,1,0:T(8,128)} %param.4) | copy-start | bytes 6291460
  361.9 8.5 %collective-permute-start.17 = (f32[34,1,512]{2,0,1:T(8,128)S(1)}, f32[34,1,512]{2,0,1:T(8,128)S(1)}, u32[]{:S(2)}, u32[]{:S(2)}) collective-permute-start(f32[34,1,512]{2,0,1:T(8,128)S(1)} %get-tuple-element.33), channel_id=1, source_target_pairs={{1,0},{2,1},{3,2},{4,3},{5,4},{6,5},{7,6},{9,8},{10,9},{11,10},{12... | collective-permute-start | bytes 208904 | tf_op jit(solution)/shard_map/ppermute | solution.py:24
  382.7 36.1 %copy-start.21 = (f32[32,32,512]{2,0,1:T(8,128)S(1)}, f32[32,32,512]{2,0,1:T(8,128)}, u32[]{:S(2)}) copy-start(f32[32,32,512]{2,0,1:T(8,128)} %fusion.11) | copy-start | bytes 6291460
  463.8 8.9 %copy-start.19 = (f32[32,32,512]{2,0,1:T(8,128)S(1)}, f32[32,32,512]{2,0,1:T(8,128)}, u32[]{:S(2)}) copy-start(f32[32,32,512]{2,0,1:T(8,128)} %copy-done.18) | copy-start | bytes 6291460
  465.0 113.3 %all-to-all-start = ((f32[1,64,16,256]{3,2,0,1:T(8,128)}), f32[1,64,16,256]{3,2,0,1:T(8,128)}, u32[]{:S(2)}, u32[]{:S(2)}) async-start(f32[1,64,16,256]{3,2,0,1:T(8,128)} %fusion.75), calls=%async_computation | async-start | bytes 2097152 | tf_op jit(solution)/shard_map/all_to_all | solution.py:182
  547.8 3.1 copy-start.25
  554.3 3.4 copy-start.26
  554.3 3.5 copy-start.24
  568.2 2.5 copy-start.27
  568.2 2.5 copy-start.28
  578.3 8.4 %copy-start.5 = (f32[32,32,512]{2,0,1:T(8,128)S(1)}, f32[32,32,512]{2,0,1:T(8,128)}, u32[]{:S(2)}) copy-start(f32[32,32,512]{2,0,1:T(8,128)} %copy-done.4) | copy-start | bytes 6291460
  578.3 66.0 %all-to-all-start.1 = ((f32[4,64,16,256]{3,2,0,1:T(8,128)}), f32[4,64,16,256]{3,2,0,1:T(8,128)}, u32[]{:S(2)}, u32[]{:S(2)}) async-start(f32[4,64,16,256]{3,2,0,1:T(8,128)} %select_bitcast_fusion), calls=%async_computation.1 | async-start | bytes 8388608 | tf_op jit(solution)/shard_map/all_to_all | solution.py:183
where the time goes:
time: 662 us; the launch traced here: 654 us
  local copies, waits for them, and re-layouts  415 us (63%)
  other arithmetic  87.8 us (13%)
  starting transfers between devices  78.7 us (12%)
  waiting for transfers between devices  70.5 us (11%)
    slice x8, local copies, waits for them, and re-layouts, pair_sum_z(): return field[..., 0::2] + field[..., 1::2]  286 us
    all_to_all x1, waiting for transfers between devices, local(): lax.all_to_all(coef_send, 'gx', split_axis=1, concat_axis=1, tiled=True)  52.5 us
    add x3, other arithmetic, smooth_each(): solution = solution + update  44.2 us
    slice x1, local copies, waits for them, and re-layouts, average_faces(): along_z = jnp.sum(split_major(faces[2][..., 0::2]), axis=(1, 3)) * 0.25  36.5 us
    ppermute x8, starting transfers between devices, padded_2(): lax.ppermute(head, axis, [((i + 1) % count, i) for i in range(ends)])  30.3 us
    ppermute x8, starting transfers between devices, padded_2(): lax.ppermute(tail, axis, [(i, (i + 1) % count) for i in range(ends)])  25.6 us
    ppermute x8, waiting for transfers between devices, padded_2(): lax.ppermute(head, axis, [((i + 1) % count, i) for i in range(ends)])  18 us
    slice x4, local copies, waits for them, and re-layouts, shift_lower(): field[..., :-1]  13.4 us
  transfers between devices with their start and end apart: 20, of which 4 were waited for; matrix products, arithmetic and copies ran while one was open for 51% of the time, Pallas kernels for 0%

commit v1 on v0

--- a/solution.py
+++ b/solution.py
@@ -104,8 +104,20 @@
     return (solution, residual)
 
 
-def pair_sum_z(field):
-    return field[..., 0::2] + field[..., 1::2]
+def z_matrix(cells, even_only):
+    fine = lax.broadcasted_iota(jnp.int32, (cells, cells // 2), 0)
+    coarse = lax.broadcasted_iota(jnp.int32, (cells, cells // 2), 1)
+    hit = fine // 2 == coarse
+    if even_only:
+        hit = hit & (fine % 2 == 0)
+    return hit.astype(jnp.float32)
+
+
+def restrict_z(field, even_only=False):
+    cells = field.shape[-1]
+    flat = field.reshape(-1, cells)
+    summed = jnp.dot(flat, z_matrix(cells, even_only), precision=lax.Precision.HIGHEST)
+    return summed.reshape(field.shape[:-1] + (cells // 2,))
 
 
 def split_major(field):
@@ -113,13 +125,13 @@
 
 
 def average_cells(field):
-    return jnp.sum(split_major(pair_sum_z(field)), axis=(1, 3)) * 0.125
+    return restrict_z(jnp.sum(split_major(field), axis=(1, 3))) * 0.125
 
 
 def average_faces(faces):
-    along_x = jnp.sum(split_major(pair_sum_z(faces[0]))[:, 0], axis=2) * 0.25
-    along_y = jnp.sum(split_major(pair_sum_z(faces[1]))[:, :, :, 0], axis=1) * 0.25
-    along_z = jnp.sum(split_major(faces[2][..., 0::2]), axis=(1, 3)) * 0.25
+    along_x = restrict_z(jnp.sum(split_major(faces[0])[:, 0], axis=2)) * 0.25
+    along_y = restrict_z(jnp.sum(split_major(faces[1])[:, :, :, 0], axis=1)) * 0.25
+    along_z = restrict_z(jnp.sum(split_major(faces[2]), axis=(1, 3)), even_only=True) * 0.25
     return [along_x, along_y, along_z]
 
 

time: 662 us -> 349 us (0.53)
  local copies, waits for them, and re-layouts: 415 us -> 100 us
  matrix products: 0 us -> 6.81 us
    slice x10 -> x1, local copies, waits for them, and re-layouts: 323 us -> 0.07 us  [the longest x8 286 us: pair_sum_z(): return field[..., 0::2] + field[..., 1::2]]
    reshape x0 -> x10, local copies, waits for them, and re-layouts: none -> 15.9 us  [coarse_tiles(): coarse.reshape(coarse.shape[0], coarse.shape[1], tiles_dev, half_cells)]
    another operation x1 -> x6, local copies, waits for them, and re-layouts: 0.12 us -> 15.1 us  [the longest x5 15 us: split_major(): field.reshape(field.shape[0] // 2, 2, field.shape[1] // 2, 2, field.shape...]
    transpose x5 -> x0, local copies, waits for them, and re-layouts: 12.9 us -> none  [coarse_tiles(): shaped.transpose(2, 1, 0, 3)]
    dot_general x0 -> x5, matrix products: none -> 6.81 us  [restrict_z(): jnp.dot(flat, z_matrix(cells, even_only), precision=lax.Precision.HIGHEST)]
  transfers between devices with their start and end apart: 20 -> 20, of which waited for: 4 -> 4; matrix products, arithmetic and copies ran while one was open for 51% -> 28% of each run, Pallas kernels for 0% -> 0%
where the time goes in v1:
time: 349 us; the launch traced here: 346 us
  local copies, waits for them, and re-layouts  100 us (29%)
  other arithmetic  89.1 us (26%)
  starting transfers between devices  80.4 us (23%)
  waiting for transfers between devices  67.5 us (19%)
  matrix products  6.81 us (2%)
    all_to_all x1, waiting for transfers between devices, local(): lax.all_to_all(coef_send, 'gx', split_axis=1, concat_axis=1, tiled=True)  52.5 us
    add x3, other arithmetic, smooth_each(): solution = solution + update  46.2 us
    ppermute x8, starting transfers between devices, padded_2(): lax.ppermute(head, axis, [((i + 1) % count, i) for i in range(ends)])  30.3 us
    ppermute x8, starting transfers between devices, padded_2(): lax.ppermute(tail, axis, [(i, (i + 1) % count) for i in range(ends)])  26.7 us
    reshape x10, local copies, waits for them, and re-layouts, coarse_tiles(): coarse.reshape(coarse.shape[0], coarse.shape[1], tiles_dev, half_cells)  15.9 us
    ppermute x8, waiting for transfers between devices, padded_2(): lax.ppermute(head, axis, [((i + 1) % count, i) for i in range(ends)])  15 us
    another operation x5, local copies, waits for them, and re-layouts, split_major(): field.reshape(field.shape[0] // 2, 2, field.shape[1] // 2, 2, field.shape...  15 us
    sub x1, other arithmetic, smooth_each(): right_side - apply_operator(field_with_rim(solution), alpha_coef, faces_p...  11.8 us
  transfers between devices with their start and end apart: 20, of which 4 were waited for; matrix products, arithmetic and copies ran while one was open for 28% of the time, Pallas kernels for 0%

profile of v1, /device:TPU:29, one launch (start us, length us, event | category | flops | bytes accessed | tf_op | source)
XLA Modules:
  0.0 345.9 jit_solution(212598681998285098)
XLA Ops:
  2.2 2.6 collective-permute-start
  6.5 5.8 %collective-permute-start.1 = (f32[32,1,512]{2,0,1:T(8,128)}, f32[32,1,512]{2,0,1:T(8,128)S(1)}, u32[]{:S(2)}, u32[]{:S(2)}) collective-permute-start(f32[32,1,512]{2,0,1:T(8,128)} %bitcast.175), channel_id=1, source_target_pairs={{1,0},{2,1},{3,2},{4,3},{5,4},{6,5},{7,6},{9,8},{10,9},{11,10},{12... | collective-permute-start | bytes 196616 | tf_op jit(solution)/shard_map/ppermute | solution.py:34
  12.9 6.1 %fusion.113 = (f32[1,32,32,512]{3,2,1,0:T(8,128)}, f32[1,32,32,512]{3,2,1,0:T(8,128)}, f32[1,32,32,512]{3,2,1,0:T(8,128)}) fusion(f32[3,32,32,512]{3,2,1,0:T(8,128)} %param.6), kind=kLoop, calls=%fused_computation.232 | loop fusion | bytes 12582912 | tf_op jit(solution)/shard_map/slice | solution.py:84
  19.8 2.2 reshape.226
  22.0 3.0 reshape.273
  25.0 1.6 copy.135
  28.1 3.3 reduce_sum.95
  32.7 2.2 convolution_multiply_fusion.2
  34.9 4.0 %copy_bitcast_fusion.7 = (f32[32,32,512]{2,0,1:T(8,128)S(1)}, f32[32,32,512]{2,0,1:T(8,128)S(1)}) fusion(f32[1,32,32,512]{3,2,1,0:T(8,128)S(1)} %copy-done.19, f32[1,32,32,512]{3,2,1,0:T(8,128)} %get-tuple-element.27), kind=kLoop, calls=%fused_computation.228 | loop fusion | bytes 8388608 | tf_op jit(solution)/shard_map/squeeze | solution.py:86
  46.8 7.7 %broadcast_multiply_fusion = (f32[32,32,512]{2,0,1:T(8,128)S(1)}, f32[32,32,512]{2,0,1:T(8,128)}) fusion(f32[32,32,512]{2,1,0:T(8,128)S(1)} %copy-done.16, f32[32,32,511]{2,0,1:T(8,128)S(1)} %slice.277, f32[1,34,34,512]{3,1,2,0:T(8,128)S(1)} %pad_bitcast_fusion, f32[1,34,34,512]{3,1,2,0:T(8,128)S(1)} %fusion.2, f32[1,34,34,512]{3,1,2,0:T(8,128)S(1)} %fusion.3, ...), kind=kLoop, calls=%fused_computation.141 | loop fusion | flops 4718592 | bytes 20967424 | tf_op jit(solution)/shard_map/div | solution.py:94
  55.9 6.3 %collective-permute-start.2 = (f32[1,32,512]{2,0,1:T(1,128)S(1)}, f32[1,32,512]{2,0,1:T(1,128)S(1)}, u32[]{:S(2)}, u32[]{:S(2)}) collective-permute-start(f32[1,32,512]{2,0,1:T(1,128)S(1)} %get-tuple-element.49), channel_id=1, source_target_pairs={{0,8},{8,16},{16,24},{24,32},{32,40},{40,48},{48,56},{56,64},{64,7... | collective-permute-start | bytes 196616 | tf_op jit(solution)/shard_map/ppermute | solution.py:22
  62.2 1.9 collective-permute-start.3
  64.2 3.5 %reshape.272 = f32[16,2,16,2,512]{4,3,2,1,0:T(2,128)} reshape(f32[1,32,32,512]{3,2,1,0:T(8,128)} %get-tuple-element.27) | data formatting | bytes 4194304 | tf_op jit(solution)/shard_map/reshape;squeeze | solution.py:124
  67.6 4.7 %copy.134 = f32[16,2,16,2,512]{4,1,0,3,2:T(2,128)} copy(f32[16,2,16,2,512]{4,3,2,1,0:T(2,128)} %reshape.272) | data formatting | bytes 4194304 | tf_op jit(solution)/shard_map/reshape;squeeze | solution.py:124
  72.3 2.1 collective-permute-start.4
  74.4 5.7 %collective-permute-start.5 = (f32[34,1,512]{2,0,1:T(8,128)S(1)}, f32[34,1,512]{2,0,1:T(8,128)S(1)}, u32[]{:S(2)}, u32[]{:S(2)}) collective-permute-start(f32[34,1,512]{2,0,1:T(8,128)S(1)} %get-tuple-element.36), channel_id=1, source_target_pairs={{1,0},{2,1},{3,2},{4,3},{5,4},{6,5},{7,6},{9,8},{10,9},{11,10},{12... | collective-permute-start | bytes 208904 | tf_op jit(solution)/shard_map/ppermute | solution.py:24
  80.2 2.7 fusion.121
  82.9 16.4 %fusion.76 = (f32[32,32,512]{2,0,1:T(8,128)}, f32[32,32,512]{2,0,1:T(8,128)}) fusion(f32[32,32,512]{2,0,1:T(8,128)} %get-tuple-element.25, f32[32,32,512]{2,0,1:T(8,128)} %copy-done.13, f32[32,32,511]{2,0,1:T(8,128)} %get-tuple-element.52, f32[32,32,511]{2,0,1:T(8,128)} %get-tuple-element.51, f32[34,1,512]{2,0,1:T(8,128)S(1)} %collective-permute-done.5, ...), kind=kLoop, calls=%fused_computation.142 | loop fusion | flops 21495808 | bytes 29618176 | tf_op jit(solution)/shard_map/add | solution.py:101
  100.8 6.6 %collective-permute-start.6 = (f32[1,32,512]{2,0,1:T(1,128)S(1)}, f32[1,32,512]{2,0,1:T(1,128)S(1)}, u32[]{:S(2)}, u32[]{:S(2)}) collective-permute-start(f32[1,32,512]{2,0,1:T(1,128)S(1)} %get-tuple-element.45), channel_id=1, source_target_pairs={{0,8},{8,16},{16,24},{24,32},{32,40},{40,48},{48,56},{56,64},{64,7... | collective-permute-start | bytes 196616 | tf_op jit(solution)/shard_map/ppermute | solution.py:22
  107.4 1.9 collective-permute-start.7
  109.3 3.0 slice_reduce_fusion
  112.3 3.0 collective-permute-done.7
  116.3 1.9 collective-permute-start.8
  118.2 5.5 %collective-permute-start.9 = (f32[34,1,512]{2,0,1:T(8,128)S(1)}, f32[34,1,512]{2,0,1:T(8,128)S(1)}, u32[]{:S(2)}, u32[]{:S(2)}) collective-permute-start(f32[34,1,512]{2,0,1:T(8,128)S(1)} %get-tuple-element.34), channel_id=1, source_target_pairs={{1,0},{2,1},{3,2},{4,3},{5,4},{6,5},{7,6},{9,8},{10,9},{11,10},{12... | collective-permute-start | bytes 208904 | tf_op jit(solution)/shard_map/ppermute | solution.py:24
  123.7 2.8 fusion.119
  126.5 15.9 %fusion.109 = (f32[32,32,512]{2,0,1:T(8,128)}, f32[32,32,512]{2,0,1:T(8,128)}) fusion(f32[32,32,512]{2,0,1:T(8,128)} %get-tuple-element.22, f32[32,32,511]{2,0,1:T(8,128)} %get-tuple-element.48, f32[32,32,511]{2,0,1:T(8,128)} %get-tuple-element.47, f32[34,1,512]{2,0,1:T(8,128)S(1)} %collective-permute-done.9, f32[1,32,512]{2,0,1:T(1,128)S(1)} %collective-permute-done.7, ...), kind=kLoop, calls=%fused_computation.231 | loop fusion | flops 20971520 | bytes 29618176 | tf_op jit(solution)/shard_map/add | solution.py:101
  143.8 3.6 %collective-permute-start.10 = (f32[1,32,512]{2,0,1:T(1,128)S(1)}, f32[1,32,512]{2,0,1:T(1,128)S(1)}, u32[]{:S(2)}, u32[]{:S(2)}) collective-permute-start(f32[1,32,512]{2,0,1:T(1,128)S(1)} %get-tuple-element.43), channel_id=1, source_target_pairs={{0,8},{8,16},{16,24},{24,32},{32,40},{40,48},{48,56},{56,64},{64,7... | collective-permute-start | bytes 196616 | tf_op jit(solution)/shard_map/ppermute | solution.py:22
  147.4 1.9 collective-permute-start.11
  149.4 6.0 %collective-permute-done.11 = f32[1,32,512]{2,0,1:T(1,128)S(1)} collective-permute-done((f32[1,32,512]{2,0,1:T(1,128)S(1)}, f32[1,32,512]{2,0,1:T(1,128)S(1)}, u32[]{:S(2)}, u32[]{:S(2)}) %collective-permute-start.11) | collective-permute-done | bytes 65568 | tf_op jit(solution)/shard_map/ppermute | solution.py:24
  156.3 1.9 collective-permute-start.12
  158.2 5.6 %collective-permute-start.13 = (f32[34,1,512]{2,0,1:T(8,128)S(1)}, f32[34,1,512]{2,0,1:T(8,128)S(1)}, u32[]{:S(2)}, u32[]{:S(2)}) collective-permute-start(f32[34,1,512]{2,0,1:T(8,128)S(1)} %get-tuple-element.32), channel_id=1, source_target_pairs={{1,0},{2,1},{3,2},{4,3},{5,4},{6,5},{7,6},{9,8},{10,9},{11,10},{12... | collective-permute-start | bytes 208904 | tf_op jit(solution)/shard_map/ppermute | solution.py:24
  163.9 2.8 fusion.116
  166.7 14.0 %fusion.29 = f32[32,32,512]{2,0,1:T(8,128)S(1)} fusion(f32[32,32,512]{2,0,1:T(8,128)} %get-tuple-element.20, f32[34,1,512]{2,0,1:T(8,128)S(1)} %collective-permute-done.13, f32[1,32,512]{2,0,1:T(1,128)S(1)} %collective-permute-done.11, f32[1,32,512]{2,0,1:T(1,128)S(1)} %collective-permute-done.10, f32[34,1,512]{2,0,1:T(8,128)S(1)} %collective-permute-done.12, ...), kind=kLoop, calls=%fused_computation.50 | loop fusion | flops 20971520 | bytes 27521024 | tf_op jit(solution)/shard_map/add | solution.py:101
  180.8 2.4 collective-permute-start.14
  183.2 1.9 collective-permute-start.15
  185.2 6.0 %collective-permute-done.15 = f32[1,32,512]{2,0,1:T(1,128)S(1)} collective-permute-done((f32[1,32,512]{2,0,1:T(1,128)S(1)}, f32[1,32,512]{2,0,1:T(1,128)S(1)}, u32[]{:S(2)}, u32[]{:S(2)}) %collective-permute-start.15) | collective-permute-done | bytes 65568 | tf_op jit(solution)/shard_map/ppermute | solution.py:24
  191.2 1.9 collective-permute-start.16
  193.2 5.7 %collective-permute-start.17 = (f32[34,1,512]{2,0,1:T(8,128)S(1)}, f32[34,1,512]{2,0,1:T(8,128)S(1)}, u32[]{:S(2)}, u32[]{:S(2)}) collective-permute-start(f32[34,1,512]{2,0,1:T(8,128)S(1)} %get-tuple-element.30), channel_id=1, source_target_pairs={{1,0},{2,1},{3,2},{4,3},{5,4},{6,5},{7,6},{9,8},{10,9},{11,10},{12... | collective-permute-start | bytes 208904 | tf_op jit(solution)/shard_map/ppermute | solution.py:24
  198.9 2.8 fusion.114
  201.8 11.8 %fusion.11 = f32[32,32,512]{2,0,1:T(8,128)} fusion(f32[32,32,512]{2,0,1:T(8,128)S(1)} %fusion.29, f32[34,1,512]{2,0,1:T(8,128)S(1)} %collective-permute-done.17, f32[1,32,512]{2,0,1:T(1,128)S(1)} %collective-permute-done.15, f32[1,32,512]{2,0,1:T(1,128)S(1)} %collective-permute-done.14, f32[34,1,512]{2,0,1:T(8,128)S(1)} %collective-permute-done.16, ...), kind=kLoop, calls=%fused_computation.24 | loop fusion | flops 14680064 | bytes 25423872 | tf_op jit(solution)/shard_map/sub | solution.py:103
  213.5 2.5 reshape.224
  216.0 1.5 reduce_sum.91
  219.1 2.6 copy.147
  221.6 2.4 reshape.232
  225.9 7.7 %all-to-all-start = ((f32[1,64,16,256]{3,2,0,1:T(8,128)}), f32[1,64,16,256]{3,2,0,1:T(8,128)}, u32[]{:S(2)}, u32[]{:S(2)}) async-start(f32[1,64,16,256]{3,2,0,1:T(8,128)} %fusion.75), calls=%async_computation | async-start | bytes 2097152 | tf_op jit(solution)/shard_map/all_to_all | solution.py:194
  233.6 1.5 convolution_multiply_fusion.1
  235.1 2.2 reshape.271
  238.0 2.5 copy.146
  240.5 2.5 stack_reshape.12
  243.7 2.5 copy.145
  246.2 2.5 stack_reshape.13
  249.4 2.5 copy.144
  251.9 2.8 stack_reshape.14
  254.7 1.5 reduce_sum.98
  258.2 2.6 copy.143
  260.8 2.4 stack_reshape.15
  263.3 2.8 gather_fusion.2
  266.2 4.7 %select_bitcast_fusion = f32[4,64,16,256]{3,2,0,1:T(8,128)} fusion(f32[64,4,16,256]{3,2,1,0:T(8,128)} %gather_fusion.2, pred[64]{0:T(512)(128)(4,1)S(1)} %fusion.95, pred[64]{0:T(512)(128)(4,1)S(1)} %copy-done.28), kind=kLoop, calls=%fused_computation.4 | loop fusion | flops 2097152 | bytes 8388736 | tf_op jit(solution)/shard_map/jit(_where)/select_n | solution.py:176
  270.9 7.4 %all-to-all-start.1 = ((f32[4,64,16,256]{3,2,0,1:T(8,128)}), f32[4,64,16,256]{3,2,0,1:T(8,128)}, u32[]{:S(2)}, u32[]{:S(2)}) async-start(f32[4,64,16,256]{3,2,0,1:T(8,128)} %select_bitcast_fusion), calls=%async_computation.1 | async-start | bytes 8388608 | tf_op jit(solution)/shard_map/all_to_all | solution.py:195
  279.3 2.5 copy.98
  281.8 1.8 gather_fusion.1
  284.4 52.5 %all-to-all-done.1 = f32[4,64,16,256]{3,2,0,1:T(8,128)} async-done(((f32[4,64,16,256]{3,2,0,1:T(8,128)}), f32[4,64,16,256]{3,2,0,1:T(8,128)}, u32[]{:S(2)}, u32[]{:S(2)}) %all-to-all-start.1) | async-done | bytes 4194336 | tf_op jit(solution)/shard_map/all_to_all | solution.py:195
  336.9 4.8 %copy.97 = f32[4,64,16,256]{3,2,1,0:T(8,128)} copy(f32[4,64,16,256]{3,2,0,1:T(8,128)} %all-to-all-done.1) | data formatting | bytes 8388608 | tf_op jit(solution)/shard_map/all_to_all | solution.py:195
  341.7 2.8 gather_fusion.3
  (139 shorter events, 31.9 us)
Async XLA Ops:
  2.2 41.7 %collective-permute-start = (f32[1,32,512]{2,0,1:T(1,128)}, f32[1,32,512]{2,0,1:T(1,128)S(1)}, u32[]{:S(2)}, u32[]{:S(2)}) collective-permute-start(f32[1,32,512]{2,0,1:T(1,128)} %bitcast.176), channel_id=1, source_target_pairs={{8,0},{16,8},{24,16},{32,24},{40,32},{48,40},{56,48},{64,56},{72,6... | collective-permute-start | bytes 196616 | tf_op jit(solution)/shard_map/ppermute | solution.py:34
  6.5 37.8 %collective-permute-start.1 = (f32[32,1,512]{2,0,1:T(8,128)}, f32[32,1,512]{2,0,1:T(8,128)S(1)}, u32[]{:S(2)}, u32[]{:S(2)}) collective-permute-start(f32[32,1,512]{2,0,1:T(8,128)} %bitcast.175), channel_id=1, source_target_pairs={{1,0},{2,1},{3,2},{4,3},{5,4},{6,5},{7,6},{9,8},{10,9},{11,10},{12... | collective-permute-start | bytes 196616 | tf_op jit(solution)/shard_map/ppermute | solution.py:34
  12.9 6.1 %copy-start.29 = (s32[1,256]{1,0:T(1,128)S(1)}, s32[1,256]{1,0:T(1,128)}, u32[]{:S(2)}) copy-start(s32[1,256]{1,0:T(1,128)} %param.7) | copy-start | bytes 3076
  12.9 6.9 %copy-start.6 = (f32[32,32,512]{2,1,0:T(8,128)S(1)}, f32[32,32,512]{2,1,0:T(8,128)}, u32[]{:S(2)}) copy-start(f32[32,32,512]{2,1,0:T(8,128)} %param.5) | copy-start | bytes 6291460
  19.0 3.0 copy-start.25
  28.1 6.8 %copy-start.19 = (f32[1,32,32,512]{3,2,1,0:T(8,128)S(1)}, f32[1,32,32,512]{3,2,1,0:T(8,128)}, u32[]{:S(2)}) copy-start(f32[1,32,32,512]{3,2,1,0:T(8,128)} %get-tuple-element.28) | copy-start | bytes 6291460
  39.4 5.6 %copy-start.2 = (f32[1,34,34,512]{3,1,2,0:T(8,128)}, f32[1,34,34,512]{3,1,2,0:T(8,128)S(1)}, u32[]{:S(2)}) copy-start(f32[1,34,34,512]{3,1,2,0:T(8,128)S(1)} %pad_bitcast_fusion) | copy-start | bytes 7102468
  39.4 0.6 copy-start.26
  39.4 0.7 copy-start.27
  39.4 2.6 copy-start.18
  43.8 1.4 copy-start.9
  44.3 1.9 copy-start.7
  44.3 2.5 copy-start.16
  46.8 7.7 %copy-start = (f32[1,34,34,512]{3,1,2,0:T(8,128)}, f32[1,34,34,512]{3,1,2,0:T(8,128)S(1)}, u32[]{:S(2)}) copy-start(f32[1,34,34,512]{3,1,2,0:T(8,128)S(1)} %fusion.2) | copy-start | bytes 7102468
  54.5 1.4 copy-start.13
  55.9 16.3 %collective-permute-start.2 = (f32[1,32,512]{2,0,1:T(1,128)S(1)}, f32[1,32,512]{2,0,1:T(1,128)S(1)}, u32[]{:S(2)}, u32[]{:S(2)}) collective-permute-start(f32[1,32,512]{2,0,1:T(1,128)S(1)} %get-tuple-element.49), channel_id=1, source_target_pairs={{0,8},{8,16},{16,24},{24,32},{32,40},{40,48},{48,56},{56,64},{64,7... | collective-permute-start | bytes 196616 | tf_op jit(solution)/shard_map/ppermute | solution.py:22
  62.2 10.1 %collective-permute-start.3 = (f32[1,32,512]{2,0,1:T(1,128)S(1)}, f32[1,32,512]{2,0,1:T(1,128)S(1)}, u32[]{:S(2)}, u32[]{:S(2)}) collective-permute-start(f32[1,32,512]{2,0,1:T(1,128)S(1)} %get-tuple-element.50), channel_id=1, source_target_pairs={{8,0},{16,8},{24,16},{32,24},{40,32},{48,40},{56,48},{64,56},{72,6... | collective-permute-start | bytes 196616 | tf_op jit(solution)/shard_map/ppermute | solution.py:24
  67.6 4.7 %copy-start.14 = (f32[32,32,512]{2,0,1:T(8,128)S(1)}, f32[32,32,512]{2,0,1:T(8,128)}, u32[]{:S(2)}) copy-start(f32[32,32,512]{2,0,1:T(8,128)} %copy-done.13) | copy-start | bytes 6291460
  72.3 10.6 %copy-start.10 = (f32[32,32,511]{2,0,1:T(8,128)S(1)}, f32[32,32,511]{2,0,1:T(8,128)}, u32[]{:S(2)}) copy-start(f32[32,32,511]{2,0,1:T(8,128)} %copy-done.9) | copy-start | bytes 6279172
  72.3 10.6 %collective-permute-start.4 = (f32[34,1,512]{2,0,1:T(8,128)S(1)}, f32[34,1,512]{2,0,1:T(8,128)S(1)}, u32[]{:S(2)}, u32[]{:S(2)}) collective-permute-start(f32[34,1,512]{2,0,1:T(8,128)S(1)} %get-tuple-element.35), channel_id=1, source_target_pairs={{0,1},{1,2},{2,3},{3,4},{4,5},{5,6},{6,7},{8,9},{9,10},{10,11},{11... | collective-permute-start | bytes 208904 | tf_op jit(solution)/shard_map/ppermute | solution.py:22
  74.4 8.5 %copy-start.3 = (f32[1,34,34,512]{3,1,2,0:T(8,128)S(1)}, f32[1,34,34,512]{3,1,2,0:T(8,128)}, u32[]{:S(2)}) copy-start(f32[1,34,34,512]{3,1,2,0:T(8,128)} %copy-done.2) | copy-start | bytes 7102468
  74.4 8.5 %copy-start.8 = (f32[32,32,512]{2,1,0:T(8,128)S(1)}, f32[32,32,512]{2,1,0:T(8,128)}, u32[]{:S(2)}) copy-start(f32[32,32,512]{2,1,0:T(8,128)} %param.5) | copy-start | bytes 6291460
  74.4 8.5 %collective-permute-start.5 = (f32[34,1,512]{2,0,1:T(8,128)S(1)}, f32[34,1,512]{2,0,1:T(8,128)S(1)}, u32[]{:S(2)}, u32[]{:S(2)}) collective-permute-start(f32[34,1,512]{2,0,1:T(8,128)S(1)} %get-tuple-element.36), channel_id=1, source_target_pairs={{1,0},{2,1},{3,2},{4,3},{5,4},{6,5},{7,6},{9,8},{10,9},{11,10},{12... | collective-permute-start | bytes 208904 | tf_op jit(solution)/shard_map/ppermute | solution.py:24
  80.2 2.8 copy-start.1
  99.3 24.4 %copy-start.12 = (f32[32,32,512]{2,0,1:T(8,128)S(1)}, f32[32,32,512]{2,0,1:T(8,128)}, u32[]{:S(2)}) copy-start(f32[32,32,512]{2,0,1:T(8,128)} %get-tuple-element.22) | copy-start | bytes 6291460
  100.8 11.6 %collective-permute-start.6 = (f32[1,32,512]{2,0,1:T(1,128)S(1)}, f32[1,32,512]{2,0,1:T(1,128)S(1)}, u32[]{:S(2)}, u32[]{:S(2)}) collective-permute-start(f32[1,32,512]{2,0,1:T(1,128)S(1)} %get-tuple-element.45), channel_id=1, source_target_pairs={{0,8},{8,16},{16,24},{24,32},{32,40},{40,48},{48,56},{56,64},{64,7... | collective-permute-start | bytes 196616 | tf_op jit(solution)/shard_map/ppermute | solution.py:22
  107.4 8.0 %collective-permute-start.7 = (f32[1,32,512]{2,0,1:T(1,128)S(1)}, f32[1,32,512]{2,0,1:T(1,128)S(1)}, u32[]{:S(2)}, u32[]{:S(2)}) collective-permute-start(f32[1,32,512]{2,0,1:T(1,128)S(1)} %get-tuple-element.46), channel_id=1, source_target_pairs={{8,0},{16,8},{24,16},{32,24},{40,32},{48,40},{56,48},{64,56},{72,6... | collective-permute-start | bytes 196616 | tf_op jit(solution)/shard_map/ppermute | solution.py:24
  116.3 10.2 %collective-permute-start.8 = (f32[34,1,512]{2,0,1:T(8,128)S(1)}, f32[34,1,512]{2,0,1:T(8,128)S(1)}, u32[]{:S(2)}, u32[]{:S(2)}) collective-permute-start(f32[34,1,512]{2,0,1:T(8,128)S(1)} %get-tuple-element.33), channel_id=1, source_target_pairs={{0,1},{1,2},{2,3},{3,4},{4,5},{5,6},{6,7},{8,9},{9,10},{10,11},{11... | collective-permute-start | bytes 208904 | tf_op jit(solution)/shard_map/ppermute | solution.py:22
  118.2 8.3 %collective-permute-start.9 = (f32[34,1,512]{2,0,1:T(8,128)S(1)}, f32[34,1,512]{2,0,1:T(8,128)S(1)}, u32[]{:S(2)}, u32[]{:S(2)}) collective-permute-start(f32[34,1,512]{2,0,1:T(8,128)S(1)} %get-tuple-element.34), channel_id=1, source_target_pairs={{1,0},{2,1},{3,2},{4,3},{5,4},{6,5},{7,6},{9,8},{10,9},{11,10},{12... | collective-permute-start | bytes 208904 | tf_op jit(solution)/shard_map/ppermute | solution.py:24
  142.4 21.5 %copy-start.15 = (f32[32,32,512]{2,0,1:T(8,128)S(1)}, f32[32,32,512]{2,0,1:T(8,128)}, u32[]{:S(2)}) copy-start(f32[32,32,512]{2,0,1:T(8,128)} %get-tuple-element.20) | copy-start | bytes 6291460
  143.8 5.6 %collective-permute-start.10 = (f32[1,32,512]{2,0,1:T(1,128)S(1)}, f32[1,32,512]{2,0,1:T(1,128)S(1)}, u32[]{:S(2)}, u32[]{:S(2)}) collective-permute-start(f32[1,32,512]{2,0,1:T(1,128)S(1)} %get-tuple-element.43), channel_id=1, source_target_pairs={{0,8},{8,16},{16,24},{24,32},{32,40},{40,48},{48,56},{56,64},{64,7... | collective-permute-start | bytes 196616 | tf_op jit(solution)/shard_map/ppermute | solution.py:22
  147.4 8.0 %collective-permute-start.11 = (f32[1,32,512]{2,0,1:T(1,128)S(1)}, f32[1,32,512]{2,0,1:T(1,128)S(1)}, u32[]{:S(2)}, u32[]{:S(2)}) collective-permute-start(f32[1,32,512]{2,0,1:T(1,128)S(1)} %get-tuple-element.44), channel_id=1, source_target_pairs={{8,0},{16,8},{24,16},{32,24},{40,32},{48,40},{56,48},{64,56},{72,6... | collective-permute-start | bytes 196616 | tf_op jit(solution)/shard_map/ppermute | solution.py:24
  156.3 10.4 %collective-permute-start.12 = (f32[34,1,512]{2,0,1:T(8,128)S(1)}, f32[34,1,512]{2,0,1:T(8,128)S(1)}, u32[]{:S(2)}, u32[]{:S(2)}) collective-permute-start(f32[34,1,512]{2,0,1:T(8,128)S(1)} %get-tuple-element.31), channel_id=1, source_target_pairs={{0,1},{1,2},{2,3},{3,4},{4,5},{5,6},{6,7},{8,9},{9,10},{10,11},{11... | collective-permute-start | bytes 208904 | tf_op jit(solution)/shard_map/ppermute | solution.py:22
  158.2 8.5 %collective-permute-start.13 = (f32[34,1,512]{2,0,1:T(8,128)S(1)}, f32[34,1,512]{2,0,1:T(8,128)S(1)}, u32[]{:S(2)}, u32[]{:S(2)}) collective-permute-start(f32[34,1,512]{2,0,1:T(8,128)S(1)} %get-tuple-element.32), channel_id=1, source_target_pairs={{1,0},{2,1},{3,2},{4,3},{5,4},{6,5},{7,6},{9,8},{10,9},{11,10},{12... | collective-permute-start | bytes 208904 | tf_op jit(solution)/shard_map/ppermute | solution.py:24
  180.7 21.1 %copy-start.4 = (f32[32,32,512]{2,0,1:T(8,128)}, f32[32,32,512]{2,0,1:T(8,128)S(1)}, u32[]{:S(2)}) copy-start(f32[32,32,512]{2,0,1:T(8,128)S(1)} %fusion.29) | copy-start | bytes 6291460
  180.8 4.4 %collective-permute-start.14 = (f32[1,32,512]{2,0,1:T(1,128)S(1)}, f32[1,32,512]{2,0,1:T(1,128)S(1)}, u32[]{:S(2)}, u32[]{:S(2)}) collective-permute-start(f32[1,32,512]{2,0,1:T(1,128)S(1)} %get-tuple-element.39), channel_id=1, source_target_pairs={{0,8},{8,16},{16,24},{24,32},{32,40},{40,48},{48,56},{56,64},{64,7... | collective-permute-start | bytes 196616 | tf_op jit(solution)/shard_map/ppermute | solution.py:22
  183.2 8.0 %collective-permute-start.15 = (f32[1,32,512]{2,0,1:T(1,128)S(1)}, f32[1,32,512]{2,0,1:T(1,128)S(1)}, u32[]{:S(2)}, u32[]{:S(2)}) collective-permute-start(f32[1,32,512]{2,0,1:T(1,128)S(1)} %get-tuple-element.40), channel_id=1, source_target_pairs={{8,0},{16,8},{24,16},{32,24},{40,32},{48,40},{56,48},{64,56},{72,6... | collective-permute-start | bytes 196616 | tf_op jit(solution)/shard_map/ppermute | solution.py:24
  191.2 10.5 %collective-permute-start.16 = (f32[34,1,512]{2,0,1:T(8,128)S(1)}, f32[34,1,512]{2,0,1:T(8,128)S(1)}, u32[]{:S(2)}, u32[]{:S(2)}) collective-permute-start(f32[34,1,512]{2,0,1:T(8,128)S(1)} %get-tuple-element.29), channel_id=1, source_target_pairs={{0,1},{1,2},{2,3},{3,4},{4,5},{5,6},{6,7},{8,9},{9,10},{10,11},{11... | collective-permute-start | bytes 208904 | tf_op jit(solution)/shard_map/ppermute | solution.py:22
  193.2 8.6 %copy-start.11 = (f32[32,32,511]{2,0,1:T(8,128)S(1)}, f32[32,32,511]{2,0,1:T(8,128)}, u32[]{:S(2)}) copy-start(f32[32,32,511]{2,0,1:T(8,128)} %copy-done.9) | copy-start | bytes 6279172
  193.2 8.6 %copy-start.17 = (f32[32,32,512]{2,1,0:T(8,128)S(1)}, f32[32,32,512]{2,1,0:T(8,128)}, u32[]{:S(2)}) copy-start(f32[32,32,512]{2,1,0:T(8,128)} %param.4) | copy-start | bytes 6291460
  193.2 8.5 %collective-permute-start.17 = (f32[34,1,512]{2,0,1:T(8,128)S(1)}, f32[34,1,512]{2,0,1:T(8,128)S(1)}, u32[]{:S(2)}, u32[]{:S(2)}) collective-permute-start(f32[34,1,512]{2,0,1:T(8,128)S(1)} %get-tuple-element.30), channel_id=1, source_target_pairs={{1,0},{2,1},{3,2},{4,3},{5,4},{6,5},{7,6},{9,8},{10,9},{11,10},{12... | collective-permute-start | bytes 208904 | tf_op jit(solution)/shard_map/ppermute | solution.py:24
  216.0 1.6 copy-start.31
  221.6 3.1 copy-start.28
  224.7 10.4 %copy-start.20 = (f32[1,32,32,512]{3,2,1,0:T(8,128)S(1)}, f32[1,32,32,512]{3,2,1,0:T(8,128)}, u32[]{:S(2)}) copy-start(f32[1,32,32,512]{3,2,1,0:T(8,128)} %get-tuple-element.28) | copy-start | bytes 6291460
  225.9 7.7 %copy-start.22 = (f32[16,16,512]{2,0,1:T(8,128)S(1)}, f32[16,16,512]{2,0,1:T(8,128)}, u32[]{:S(2)}) copy-start(f32[16,16,512]{2,0,1:T(8,128)} %slice_reduce_fusion) | copy-start | bytes 1572868
  225.9 45.0 %all-to-all-start = ((f32[1,64,16,256]{3,2,0,1:T(8,128)}), f32[1,64,16,256]{3,2,0,1:T(8,128)}, u32[]{:S(2)}, u32[]{:S(2)}) async-start(f32[1,64,16,256]{3,2,0,1:T(8,128)} %fusion.75), calls=%async_computation | async-start | bytes 2097152 | tf_op jit(solution)/shard_map/all_to_all | solution.py:194
  240.5 2.5 copy-start.23
  246.2 2.5 copy-start.24
  251.9 2.8 copy-start.21
  254.7 1.9 copy-start.32
  270.9 7.4 %copy-start.30 = (s32[1,256]{1,0:T(1,128)S(1)}, s32[1,256]{1,0:T(1,128)}, u32[]{:S(2)}) copy-start(s32[1,256]{1,0:T(1,128)} %param.7) | copy-start | bytes 3076
  270.9 8.4 %copy-start.5 = (f32[32,32,512]{2,0,1:T(8,128)S(1)}, f32[32,32,512]{2,0,1:T(8,128)}, u32[]{:S(2)}) copy-start(f32[32,32,512]{2,0,1:T(8,128)} %copy-done.4) | copy-start | bytes 6291460
  270.9 66.0 %all-to-all-start.1 = ((f32[4,64,16,256]{3,2,0,1:T(8,128)}), f32[4,64,16,256]{3,2,0,1:T(8,128)}, u32[]{:S(2)}, u32[]{:S(2)}) async-start(f32[4,64,16,256]{3,2,0,1:T(8,128)} %select_bitcast_fusion), calls=%async_computation.1 | async-start | bytes 8388608 | tf_op jit(solution)/shard_map/all_to_all | solution.py:195
